TPU v7x, 32 devices: a whole 2x2x4 slice. The times are simulated.
32 devices in a mesh: ctx: 8 (over y, x, core), ch: 4 (over z).
Axes of the slice: x: 2, y: 2, z: 4, core: 2. Of those that a mesh axis runs over, the one named last changes fastest.
Arguments:
- query: float32 [1024, 6144], P('ctx', 'ch'), may hold values from -6 to 6
- key_proj: float32 [1024, 6144], P('ctx', 'ch'), may hold values from -6 to 6
- value_proj: float32 [1024, 6144], P('ctx', 'ch'), may hold values from -6 to 6
- skip_gain: float32 [6144], P('ch'), may hold values from -4 to 4
- rates: float32 [384, 16], P('ch'), as said below
- residues: float32 [384, 16], P('ch')
- w_out: bfloat16 [6144, 8192], P('ch', 'ctx'), may hold values from -0.078125 to 0.078125
Outputs:
- projected_out: float32 [1024, 8192], P('ctx', 'ch')
Inputs may be any that keep to these rules, and one draw needn't show every extreme that they name: `rates`: each rate is positive, from 0.3 / 1024 up to 1 / 24.
All inputs are finite; a program needn't handle non-finite values.
Results may differ from a plain program's by a relative error of at most 0.0029.
Values may be sent and summed in bfloat16 or wider, within the bound.
A program may use at most 192 MiB of HBM per device.

v0:
```python
import jax
import jax.numpy as jnp
from jax import lax
from jax.sharding import PartitionSpec as P

SUB = 128


def shards(query, key_proj, value_proj, skip_gain, rates, residues, w_out):
    tok_rows, chan_count = query.shape
    filter_count, mode_count = rates.shape
    group_size = chan_count // filter_count
    sub_blocks = tok_rows // SUB
    highest = lax.Precision.HIGHEST
    kv_prod = key_proj * value_proj
    blocked = kv_prod.reshape(sub_blocks, SUB, filter_count, group_size).transpose(2, 3, 0, 1)
    lag_pos = jnp.arange(SUB, dtype=jnp.float32)
    lag_decay = jnp.exp(-rates[:, :, None] * lag_pos[None, None, :])
    filter_taps = jnp.einsum("fn,fnt->ft", residues, lag_decay, precision=highest)
    offset = jnp.arange(SUB)[None, :] - jnp.arange(SUB)[:, None]
    toeplitz = jnp.where(
        offset[None] >= 0, jnp.take(filter_taps, jnp.maximum(offset, 0), axis=1), 0.0
    )
    local_out = jnp.einsum("fgkj,fji->fgki", blocked, toeplitz, precision=highest)
    end_decay = jnp.exp(-rates[:, :, None] * (SUB - 1 - lag_pos)[None, None, :])
    states = jnp.einsum("fgkj,fnj->fgkn", blocked, end_decay, precision=highest)
    sub_index = jnp.arange(sub_blocks, dtype=jnp.float32)
    sub_gap = sub_index[:, None] - 1.0 - sub_index[None, :]
    within = jnp.where(
        sub_gap[None, None] >= 0,
        jnp.exp(-rates[:, :, None, None] * SUB * jnp.maximum(sub_gap, 0.0)[None, None]),
        0.0,
    )
    prefix = jnp.einsum("fnkl,fgln->fgkn", within, states, precision=highest)
    tail_decay = jnp.exp(-rates[:, :, None] * SUB * (sub_blocks - 1 - sub_index)[None, None, :])
    own_state = jnp.einsum("fnk,fgkn->fgn", tail_decay, states, precision=highest)
    position = lax.axis_index("ctx")
    block_piece = lax.all_gather(own_state[None], "ctx", axis=0, tiled=True)
    source_rank = jnp.arange(block_piece.shape[0])
    rank_gap = (position - 1 - source_rank).astype(jnp.float32)
    weight = jnp.where(
        rank_gap[:, None, None] >= 0,
        jnp.exp(-rates[None] * tok_rows * jnp.maximum(rank_gap, 0.0)[:, None, None]),
        0.0,
    )
    incoming = jnp.einsum("jfn,jfgn->fgn", weight, block_piece, precision=highest)
    entry_decay = jnp.exp(-rates[:, :, None] * SUB * sub_index[None, None, :])
    carried = (
        prefix + incoming[:, :, None, :] * jnp.transpose(entry_decay, (0, 2, 1))[:, None, :, :]
    )
    out_decay = residues[:, :, None] * jnp.exp(-rates[:, :, None] * (lag_pos + 1.0)[None, None, :])
    cross_out = jnp.einsum("fgkn,fni->fgki", carried, out_decay, precision=highest)
    conv_out = (local_out + cross_out).transpose(2, 3, 0, 1).reshape(tok_rows, chan_count)
    hidden = (query * (conv_out + skip_gain[None, :] * kv_prod)).astype(jnp.bfloat16)
    partial_out = jnp.dot(
        hidden, lax.all_gather(w_out, "ctx", axis=1, tiled=True), preferred_element_type=jnp.float32
    )
    return lax.psum_scatter(partial_out, "ch", scatter_dimension=1, tiled=True)


def solution(mesh):
    placed = (
        P("ctx", "ch"),
        P("ctx", "ch"),
        P("ctx", "ch"),
        P("ch"),
        P("ch", None),
        P("ch", None),
        P("ch", "ctx"),
    )
    return jax.shard_map(
        shards, mesh=mesh, in_specs=placed, out_specs=P("ctx", "ch"), check_vma=False
    )
```

profile of v0, /device:TPU:0, one launch (start us, length us, event | category | flops | bytes accessed | tf_op | source)
XLA Modules:
  0.0 254.6 jit_solution(7362462676393946079)
XLA Ops:
  6.5 0.0 all-gather.3.cloned.1.call-start
  6.5 0.7 all-gather.3.cloned.1.call-update
  7.3 0.0 reduce-scatter.2.cloned.1.call-start
  7.3 0.7 broadcast_multiply_fusion
  8.0 0.1 copy.27
  8.1 1.4 copy.25
  9.5 1.4 copy.26
  10.9 0.1 copy.29
  11.0 0.1 mul.51
  11.1 1.4 fusion.18
  12.6 0.3 multiply_bitcast_fusion
  12.8 0.3 copy.30
  13.1 0.1 copy.31
  13.2 55.3 %all-gather = f32[768,16,16]{2,1,0:T(8,128)S(1)} all-gather(f32[96,16,16]{2,1,0:T(8,128)S(1)} %copy.30), channel_id=2, replica_groups=mesh['ctx'=8,'ch'=4] {'ctx'}, dimensions={0}, use_global_device_ids=true | all-gather | bytes 884736 | tf_op jit(solution)/shard_map/all_gather | solution.py:38
  68.5 0.1 select_bitcast_fusion
  68.7 0.9 multiply_reduce_fusion
  69.6 0.3 copy.46
  69.9 0.0 copy-done.1
  69.9 0.1 copy.48
  70.0 0.5 multiply_reduce_fusion.1
  70.5 0.1 copy.38
  70.6 54.5 %gather_fusion = f32[16384,96]{1,0:T(8,128)} fusion(f32[96,128]{0,1:T(8,128)S(1)} %copy.38, s32[16384]{0:T(1024)S(1)} %bitcast_clamp_fusion), kind=kCustom, calls=%fused_computation | custom fusion | bytes 12648448 | tf_op jit(solution)/shard_map/jit(_take)/gather | solution.py:22
  125.1 8.6 %copy.28 = f32[128,128,96]{1,0,2:T(8,128)} copy(f32[128,128,96]{2,1,0:T(8,128)} %bitcast.49) | data formatting | bytes 12582912 | tf_op jit(solution)/shard_map/jit(_take)/gather | solution.py:22
  133.7 1.4 copy.34
  135.2 7.6 %fusion = f32[96,16,128]{2,1,0:T(8,128)S(1)} fusion(f32[96,16,128]{2,1,0:T(8,128)S(1)} %bitcast.52, f32[128,128,96]{1,0,2:T(8,128)} %copy.28, pred[128,128]{1,0:T(8,128)(4,1)S(1)} %get-tuple-element.9, pred[128,128]{1,0:T(8,128)(4,1)S(1)} %get-tuple-element.8), kind=kOutput, calls=%fused_computation.1 | convolution fusion | flops 305135616 | bytes 7897088 | tf_op jit(solution)/shard_map/fgkj,fji->fgki/dot_general | solution.py:24
  142.8 2.1 convolution_add_fusion
  144.9 0.0 copy-done
  144.9 0.3 fusion.9
  145.2 11.9 %all-gather.3.cloned.1.call-done = bf16[1536,8192]{1,0:T(8,128)(2,1)} async-done(((bf16[1536,1024]{1,0:T(8,128)(2,1)}), bf16[1536,8192]{1,0:T(8,128)(2,1)}) %all-gather.3.cloned.1.call-update) | async-done | bytes 25165840 | tf_op jit(solution)/shard_map/all_gather | solution.py:56
  157.1 13.7 %fusion.32 = f32[128,8192]{1,0:T(8,128)} fusion(bf16[128,1536]{0,1:T(8,128)(2,1)S(1)} %fusion.9, bf16[1536,8192]{1,0:T(8,128)(2,1)} %all-gather.3.cloned.1.call-done), kind=kOutput, calls=%fused_computation.49 | convolution fusion | flops 3221225472 | bytes 29753344 | tf_op jit(solution)/shard_map/dot_general | solution.py:55
  170.8 0.0 reduce-scatter.2.cloned.1.call-update
  170.8 76.9 %reduce-scatter.2.cloned.1.call-done = f32[128,2048]{1,0:T(8,128)} async-done(((f32[128,8192]{1,0:T(8,128)}), f32[128,2048]{1,0:T(8,128)}) %reduce-scatter.2.cloned.1.call-update) | async-done | bytes 1048592 | tf_op jit(solution)/shard_map/reduce_scatter | solution.py:58
  (8 shorter events, 0.1 us)
Async XLA Ops:
  6.5 150.5 %all-gather.3.cloned.1.call-start = ((), (), s32[]{:S(2)}) async-start(), calls=%async_computation.1 | async-start | bytes 28311552 | tf_op jit(solution)/shard_map/all_gather | solution.py:56
  7.3 240.5 %reduce-scatter.2.cloned.1.call-start = ((), (), s32[]{:S(2)}) async-start(), calls=%async_computation.2 | async-start | bytes 5242880 | tf_op jit(solution)/shard_map/reduce_scatter | solution.py:58
  68.5 1.3 copy-start.1
  133.7 11.1 %copy-start = (f32[1536]{0:T(1024)S(1)}, f32[1536]{0:T(1024)}, u32[]{:S(2)}) copy-start(f32[1536]{0:T(1024)} %param.10) | copy-start | bytes 18436
Sparse Core Ops, SparseCore 0:
  9.3 147.7 all-gather.2
  170.9 76.7 reduce-scatter.1
where the time goes:
time: 255 us
  waiting for transfers between devices  89.5 us (35%)
  local copies, waits for them, and re-layouts  68.3 us (27%)
  blocking collectives  55.3 us (22%)
  matrix products  24.8 us (10%)
  between operations  13.6 us (5%)
  other arithmetic  2.99 us (1%)
    reduce_scatter x1, waiting for transfers between devices, shards(): return lax.psum_scatter(partial_out, 'ch', scatter_dimension=1, tiled=True)  76.9 us
    gather x2, local copies, waits for them, and re-layouts, shards(): jnp.take(filter_taps, jnp.maximum(offset, 0), axis=1)  63.1 us
    all_gather x1, blocking collectives, shards(): block_piece = lax.all_gather(own_state[None], 'ctx', axis=0, tiled=True)  55.3 us
    dot_general x1, matrix products, shards(): jnp.dot(hidden, lax.all_gather(w_out, 'ctx', axis=1, tiled=True), preferr...  13.7 us
    all_gather x1, waiting for transfers between devices, shards(): lax.all_gather(w_out, 'ctx', axis=1, tiled=True)  11.9 us
    dot_general x1, matrix products, shards(): jnp.einsum('fgkj,fji->fgki', blocked, toeplitz, precision=highest)  7.6 us
  transfers between devices with their start and end apart: 2, of which 2 were waited for; matrix products, arithmetic and copies ran while one was open for 32% of the time, Pallas kernels for 0%

commit v1 on v0

--- a/solution.py
+++ b/solution.py
@@ -35,7 +35,12 @@
     tail_decay = jnp.exp(-rates[:, :, None] * SUB * (sub_blocks - 1 - sub_index)[None, None, :])
     own_state = jnp.einsum("fnk,fgkn->fgn", tail_decay, states, precision=highest)
     position = lax.axis_index("ctx")
-    block_piece = lax.all_gather(own_state[None], "ctx", axis=0, tiled=True)
+    ring = [own_state[None]]
+    for hop in range(7):
+        ring.append(lax.ppermute(ring[-1], "ctx", [(dev, (dev + 1) % 8) for dev in range(8)]))
+    block_piece = jnp.roll(
+        jnp.concatenate(ring[::-1], axis=0), (lax.axis_index("ctx") + 1) * ring[0].shape[0], axis=0
+    )
     source_rank = jnp.arange(block_piece.shape[0])
     rank_gap = (position - 1 - source_rank).astype(jnp.float32)
     weight = jnp.where(

time: 255 us -> 243 us (0.953)
  blocking collectives: 55.3 us -> 0 us
  waiting for transfers between devices: 89.5 us -> 123 us
  starting transfers between devices: 0.04 us -> 5.16 us
  local copies, waits for them, and re-layouts: 68.3 us -> 72 us
    all_gather x1 -> x0, blocking collectives: 55.3 us -> none  [shards(): block_piece = lax.all_gather(own_state[None], 'ctx', axis=0, tiled=True)]
    ppermute x0 -> x7, waiting for transfers between devices: none -> 35.5 us  [shards(): lax.ppermute(ring[-1], 'ctx', [(dev, (dev + 1) % 8) for dev in range(8)])]
    ppermute x0 -> x7, starting transfers between devices: none -> 5.12 us  [shards(): lax.ppermute(ring[-1], 'ctx', [(dev, (dev + 1) % 8) for dev in range(8)])]
    unnamed x8 -> x48, local copies, waits for them, and re-layouts: 4.29 us -> 7.58 us
  transfers between devices with their start and end apart: 2 -> 9, of which waited for: 2 -> 7; matrix products, arithmetic and copies ran while one was open for 32% -> 36% of each run, Pallas kernels for 0% -> 0%
where the time goes in v1:
time: 243 us; the launch traced here: 242 us
  waiting for transfers between devices  123 us (51%)
  local copies, waits for them, and re-layouts  72 us (30%)
  matrix products  26.9 us (11%)
  between operations  13.8 us (6%)
  starting transfers between devices  5.16 us (2%)
    reduce_scatter x1, waiting for transfers between devices, shards(): return lax.psum_scatter(partial_out, 'ch', scatter_dimension=1, tiled=True)  76 us
    gather x2, local copies, waits for them, and re-layouts, shards(): jnp.take(filter_taps, jnp.maximum(offset, 0), axis=1)  63.3 us
    ppermute x7, waiting for transfers between devices, shards(): lax.ppermute(ring[-1], 'ctx', [(dev, (dev + 1) % 8) for dev in range(8)])  35.5 us
    dot_general x1, matrix products, shards(): jnp.dot(hidden, lax.all_gather(w_out, 'ctx', axis=1, tiled=True), preferr...  13.7 us
    all_gather x1, waiting for transfers between devices, shards(): lax.all_gather(w_out, 'ctx', axis=1, tiled=True)  10.8 us
    dot_general x1, matrix products, shards(): jnp.einsum('fgkj,fji->fgki', blocked, toeplitz, precision=highest)  8.39 us
    unnamed x48, local copies, waits for them, and re-layouts  7.58 us
    ppermute x7, starting transfers between devices, shards(): lax.ppermute(ring[-1], 'ctx', [(dev, (dev + 1) % 8) for dev in range(8)])  5.12 us
  transfers between devices with their start and end apart: 9, of which 7 were waited for; matrix products, arithmetic and copies ran while one was open for 36% of the time, Pallas kernels for 0%

profile of v1, /device:TPU:0, one launch (start us, length us, event | category | flops | bytes accessed | tf_op | source)
XLA Modules:
  0.0 242.4 jit_solution(5362020879108789252)
XLA Ops:
  6.5 0.7 all-gather.2.cloned.1.call-update
  7.4 0.3 copy-done
  8.0 0.3 copy.26
  8.4 1.4 fusion.18
  9.9 0.3 multiply_bitcast_fusion
  10.2 0.4 copy.30
  10.5 0.5 collective-permute-start
  11.2 0.5 multiply_reduce_fusion.1
  11.8 54.8 %gather_fusion = f32[16384,96]{1,0:T(8,128)} fusion(f32[96,128]{0,1:T(8,128)S(1)} %copy.40, s32[16384]{0:T(1024)S(1)} %bitcast_clamp_fusion), kind=kCustom, calls=%fused_computation | custom fusion | bytes 12648448 | tf_op jit(solution)/shard_map/jit(_take)/gather | solution.py:22
  66.6 8.5 %copy.28 = f32[128,128,96]{1,0,2:T(8,128)} copy(f32[128,128,96]{2,1,0:T(8,128)} %bitcast.50) | data formatting | bytes 12582912 | tf_op jit(solution)/shard_map/jit(_take)/gather | solution.py:22
  75.1 2.7 %collective-permute-start.1 = (f32[1,96,16,16]{1,3,2,0:T(8,128)S(1)}, f32[1,96,16,16]{1,3,2,0:T(8,128)S(1)}, u32[]{:S(2)}, u32[]{:S(2)}) collective-permute-start(f32[1,96,16,16]{1,3,2,0:T(8,128)S(1)} %collective-permute-done), channel_id=1, source_target_pairs={{0,4},{4,8},{8,12},{12,16},{16,20},{20,24},{24,28},{28,0},{1,5},{5... | collective-permute-start | bytes 294920 | tf_op jit(solution)/shard_map/ppermute | solution.py:40
  77.8 5.6 %collective-permute-done.1 = f32[1,96,16,16]{1,3,2,0:T(8,128)S(1)} collective-permute-done((f32[1,96,16,16]{1,3,2,0:T(8,128)S(1)}, f32[1,96,16,16]{1,3,2,0:T(8,128)S(1)}, u32[]{:S(2)}, u32[]{:S(2)}) %collective-permute-start.1) | collective-permute-done | bytes 98336 | tf_op jit(solution)/shard_map/ppermute | solution.py:40
  83.5 8.4 %fusion = f32[96,16,128]{2,1,0:T(8,128)} fusion(f32[96,16,128]{2,1,0:T(8,128)S(1)} %bitcast.52, f32[128,128,96]{1,0,2:T(8,128)} %copy.28, pred[128,128]{1,0:T(8,128)(4,1)S(1)} %get-tuple-element.9, pred[128,128]{1,0:T(8,128)(4,1)S(1)} %get-tuple-element.8), kind=kOutput, calls=%fused_computation.1 | convolution fusion | flops 305135616 | bytes 7897088 | tf_op jit(solution)/shard_map/fgkj,fji->fgki/dot_general | solution.py:24
  92.0 1.9 collective-permute-start.3
  93.9 6.3 %collective-permute-done.3 = f32[1,96,16,16]{1,3,2,0:T(8,128)S(1)} collective-permute-done((f32[1,96,16,16]{1,3,2,0:T(8,128)S(1)}, f32[1,96,16,16]{1,3,2,0:T(8,128)S(1)}, u32[]{:S(2)}, u32[]{:S(2)}) %collective-permute-start.3) | collective-permute-done | bytes 98336 | tf_op jit(solution)/shard_map/ppermute | solution.py:40
  100.2 8.2 %collective-permute-done.4 = f32[1,96,16,16]{1,3,2,0:T(8,128)} collective-permute-done((f32[1,96,16,16]{1,3,2,0:T(8,128)S(1)}, f32[1,96,16,16]{1,3,2,0:T(8,128)}, u32[]{:S(2)}, u32[]{:S(2)}) %collective-permute-start.4) | collective-permute-done | bytes 98336 | tf_op jit(solution)/shard_map/ppermute | solution.py:40
  108.6 0.8 copy.51
  109.3 0.3 copy.36
  109.6 7.2 %collective-permute-done.5 = f32[1,96,16,16]{1,3,2,0:T(8,128)} collective-permute-done((f32[1,96,16,16]{1,3,2,0:T(8,128)}, f32[1,96,16,16]{1,3,2,0:T(8,128)}, u32[]{:S(2)}, u32[]{:S(2)}) %collective-permute-start.5) | collective-permute-done | bytes 98336 | tf_op jit(solution)/shard_map/ppermute | solution.py:40
  116.8 8.3 %collective-permute-done.6 = f32[1,96,16,16]{1,3,2,0:T(8,128)S(1)} collective-permute-done((f32[1,96,16,16]{1,3,2,0:T(8,128)}, f32[1,96,16,16]{1,3,2,0:T(8,128)S(1)}, u32[]{:S(2)}, u32[]{:S(2)}) %collective-permute-start.6) | collective-permute-done | bytes 98336 | tf_op jit(solution)/shard_map/ppermute | solution.py:40
  125.1 0.9 constant_dynamic-update-slice_fusion.14
  126.0 0.9 constant_dynamic-update-slice_fusion.13
  126.9 0.9 constant_dynamic-update-slice_fusion.12
  127.9 0.9 constant_dynamic-update-slice_fusion.11
  128.9 0.9 constant_dynamic-update-slice_fusion.6
  129.8 0.9 constant_dynamic-update-slice_fusion.5
  131.0 0.4 copy.48
  131.4 3.3 %convolution_add_fusion = f32[96,16,128]{2,1,0:T(8,128)S(1)} fusion(f32[96,16,128]{2,1,0:T(8,128)} %fusion, f32[96,16,16]{2,1,0:T(8,128)S(1)} %copy.48, f32[96,16,16]{2,1,0:T(8,128)S(1)} %fusion.18, f32[96,16]{1,0:T(8,128)} %copy-done.10, f32[128]{0:T(128)S(1)} %iota_add_fusion, f32[96,16]{1,0:T(8,128)} %copy-done.8, f32[96,16]{1,0:T(8,128)} %copy-done.7), kind=kOutput, calls=%fused_computation.9 | convolution fusion | flops 38412288 | bytes 1788416 | tf_op jit(solution)/shard_map/fgkn,fni->fgki/dot_general | solution.py:57
  134.7 0.3 fusion.9
  135.0 10.8 %all-gather.2.cloned.1.call-done = bf16[1536,8192]{1,0:T(8,128)(2,1)} async-done(((bf16[1536,1024]{1,0:T(8,128)(2,1)}), bf16[1536,8192]{1,0:T(8,128)(2,1)}) %all-gather.2.cloned.1.call-update) | async-done | bytes 25165840 | tf_op jit(solution)/shard_map/all_gather | solution.py:61
  145.8 13.7 %fusion.32 = f32[128,8192]{1,0:T(8,128)} fusion(bf16[128,1536]{0,1:T(8,128)(2,1)S(1)} %fusion.9, bf16[1536,8192]{1,0:T(8,128)(2,1)} %all-gather.2.cloned.1.call-done), kind=kOutput, calls=%fused_computation.65 | convolution fusion | flops 3221225472 | bytes 29753344 | tf_op jit(solution)/shard_map/dot_general | solution.py:60
  159.5 76.0 %reduce-scatter.2.cloned.1.call-done = f32[128,2048]{1,0:T(8,128)} async-done(((f32[128,8192]{1,0:T(8,128)}), f32[128,2048]{1,0:T(8,128)}) %reduce-scatter.2.cloned.1.call-update) | async-done | bytes 1048592 | tf_op jit(solution)/shard_map/reduce_scatter | solution.py:63
  (62 shorter events, 1.4 us)
Async XLA Ops:
  6.5 0.8 copy-start.13
  6.5 1.1 copy-start
  6.5 1.4 copy-start.1
  6.5 139.2 %all-gather.2.cloned.1.call-start = ((), (), s32[]{:S(2)}) async-start(), calls=%async_computation.1 | async-start | bytes 28311552 | tf_op jit(solution)/shard_map/all_gather | solution.py:61
  7.3 228.3 %reduce-scatter.2.cloned.1.call-start = ((), (), s32[]{:S(2)}) async-start(), calls=%async_computation.2 | async-start | bytes 5242880 | tf_op jit(solution)/shard_map/reduce_scatter | solution.py:63
  7.7 3.5 %copy-start.7 = (f32[96,16]{1,0:T(8,128)}, f32[96,16]{1,0:T(8,128)S(1)}, u32[]{:S(2)}) copy-start(f32[96,16]{1,0:T(8,128)S(1)} %copy.27) | copy-start | bytes 18436
  8.3 1.6 copy-start.8
  8.4 2.6 %copy-start.12 = (f32[96,16]{0,1:T(8,128)S(1)}, f32[96,16]{0,1:T(8,128)}, u32[]{:S(2)}) copy-start(f32[96,16]{0,1:T(8,128)} %param.12) | copy-start | bytes 18436
  10.5 64.6 %collective-permute-start = (f32[1,96,16,16]{1,3,2,0:T(8,128)S(1)}, f32[1,96,16,16]{1,3,2,0:T(8,128)S(1)}, u32[]{:S(2)}, u32[]{:S(2)}) collective-permute-start(f32[1,96,16,16]{1,3,2,0:T(8,128)S(1)} %copy.30), channel_id=1, source_target_pairs={{0,4},{4,8},{8,12},{12,16},{16,20},{20,24},{24,28},{28,0},{1,5},{5... | collective-permute-start | bytes 294920 | tf_op jit(solution)/shard_map/ppermute | solution.py:40
  11.1 55.5 %copy-start.10 = (f32[96,16]{1,0:T(8,128)}, f32[96,16]{1,0:T(8,128)S(1)}, u32[]{:S(2)}) copy-start(f32[96,16]{1,0:T(8,128)S(1)} %copy.50) | copy-start | bytes 18436
  75.1 8.3 %collective-permute-start.1 = (f32[1,96,16,16]{1,3,2,0:T(8,128)S(1)}, f32[1,96,16,16]{1,3,2,0:T(8,128)S(1)}, u32[]{:S(2)}, u32[]{:S(2)}) collective-permute-start(f32[1,96,16,16]{1,3,2,0:T(8,128)S(1)} %collective-permute-done), channel_id=1, source_target_pairs={{0,4},{4,8},{8,12},{12,16},{16,20},{20,24},{24,28},{28,0},{1,5},{5... | collective-permute-start | bytes 294920 | tf_op jit(solution)/shard_map/ppermute | solution.py:40
  83.5 8.5 %collective-permute-start.2 = (f32[1,96,16,16]{1,3,2,0:T(8,128)S(1)}, f32[1,96,16,16]{1,3,2,0:T(8,128)S(1)}, u32[]{:S(2)}, u32[]{:S(2)}) collective-permute-start(f32[1,96,16,16]{1,3,2,0:T(8,128)S(1)} %collective-permute-done.1), channel_id=1, source_target_pairs={{0,4},{4,8},{8,12},{12,16},{16,20},{20,24},{24,28},{28,0},{1,5},{5... | collective-permute-start | bytes 294920 | tf_op jit(solution)/shard_map/ppermute | solution.py:40
  83.5 25.9 %copy-start.2 = (f32[128,1536]{1,0:T(8,128)S(1)}, f32[128,1536]{1,0:T(8,128)}, u32[]{:S(2)}) copy-start(f32[128,1536]{1,0:T(8,128)} %param.7) | copy-start | bytes 2359300
  91.9 16.5 %copy-start.3 = (f32[1,96,16,16]{1,3,2,0:T(8,128)}, f32[1,96,16,16]{1,3,2,0:T(8,128)S(1)}, u32[]{:S(2)}) copy-start(f32[1,96,16,16]{1,3,2,0:T(8,128)S(1)} %collective-permute-done.2) | copy-start | bytes 294916
  92.0 8.3 %collective-permute-start.3 = (f32[1,96,16,16]{1,3,2,0:T(8,128)S(1)}, f32[1,96,16,16]{1,3,2,0:T(8,128)S(1)}, u32[]{:S(2)}, u32[]{:S(2)}) collective-permute-start(f32[1,96,16,16]{1,3,2,0:T(8,128)S(1)} %collective-permute-done.2), channel_id=1, source_target_pairs={{0,4},{4,8},{8,12},{12,16},{16,20},{20,24},{24,28},{28,0},{1,5},{5... | collective-permute-start | bytes 294920 | tf_op jit(solution)/shard_map/ppermute | solution.py:40
  100.2 8.2 %copy-start.5 = (f32[1,96,16,16]{1,3,2,0:T(8,128)}, f32[1,96,16,16]{1,3,2,0:T(8,128)S(1)}, u32[]{:S(2)}) copy-start(f32[1,96,16,16]{1,3,2,0:T(8,128)S(1)} %collective-permute-done.3) | copy-start | bytes 294916
  100.2 8.2 %collective-permute-start.4 = (f32[1,96,16,16]{1,3,2,0:T(8,128)S(1)}, f32[1,96,16,16]{1,3,2,0:T(8,128)}, u32[]{:S(2)}, u32[]{:S(2)}) collective-permute-start(f32[1,96,16,16]{1,3,2,0:T(8,128)S(1)} %collective-permute-done.3), channel_id=1, source_target_pairs={{0,4},{4,8},{8,12},{12,16},{16,20},{20,24},{24,28},{28,0},{1,5},{5... | collective-permute-start | bytes 294920 | tf_op jit(solution)/shard_map/ppermute | solution.py:40
  108.4 8.4 %collective-permute-start.5 = (f32[1,96,16,16]{1,3,2,0:T(8,128)}, f32[1,96,16,16]{1,3,2,0:T(8,128)}, u32[]{:S(2)}, u32[]{:S(2)}) collective-permute-start(f32[1,96,16,16]{1,3,2,0:T(8,128)} %collective-permute-done.4), channel_id=1, source_target_pairs={{0,4},{4,8},{8,12},{12,16},{16,20},{20,24},{24,28},{28,0},{1,5},{5... | collective-permute-start | bytes 294920 | tf_op jit(solution)/shard_map/ppermute | solution.py:40
  109.6 21.1 %copy-start.6 = (f32[1,96,16,16]{1,3,2,0:T(8,128)S(1)}, f32[1,96,16,16]{1,3,2,0:T(8,128)}, u32[]{:S(2)}) copy-start(f32[1,96,16,16]{1,3,2,0:T(8,128)} %copy-done.5) | copy-start | bytes 294916
  109.6 21.1 %copy-start.4 = (f32[1,96,16,16]{1,3,2,0:T(8,128)S(1)}, f32[1,96,16,16]{1,3,2,0:T(8,128)}, u32[]{:S(2)}) copy-start(f32[1,96,16,16]{1,3,2,0:T(8,128)} %copy-done.3) | copy-start | bytes 294916
  116.8 8.3 %collective-permute-start.6 = (f32[1,96,16,16]{1,3,2,0:T(8,128)}, f32[1,96,16,16]{1,3,2,0:T(8,128)S(1)}, u32[]{:S(2)}, u32[]{:S(2)}) collective-permute-start(f32[1,96,16,16]{1,3,2,0:T(8,128)} %collective-permute-done.5), channel_id=1, source_target_pairs={{0,4},{4,8},{8,12},{12,16},{16,20},{20,24},{24,28},{28,0},{1,5},{5... | collective-permute-start | bytes 294920 | tf_op jit(solution)/shard_map/ppermute | solution.py:40
  116.8 14.0 %copy-start.9 = (f32[96,16,8]{0,1,2:T(8,128)S(1)}, f32[96,16,8]{0,1,2:T(8,128)}, u32[]{:S(2)}) copy-start(f32[96,16,8]{0,1,2:T(8,128)} %copy.51) | copy-start | bytes 147460
  131.0 3.7 %copy-start.11 = (f32[1536]{0:T(1024)S(1)}, f32[1536]{0:T(1024)}, u32[]{:S(2)}) copy-start(f32[1536]{0:T(1024)} %param.10) | copy-start | bytes 18436
Sparse Core Ops, SparseCore 0:
  9.3 136.4 all-gather.1
  159.6 75.8 reduce-scatter.1
